TPU v7x, 256 devices: a whole 4x4x8 slice. The times are simulated.
256 devices in a mesh: gx: 16 (over z, y_lo), gy: 16 (over y_hi, x, core).
Axes of the slice: x: 4, y: 4 (y_hi: 2, y_lo: 2; y = y_hi * 2 + y_lo), z: 8, core: 2. Of those that a mesh axis runs over, the one named last changes fastest.
Arguments:
- psi: float32 [64, 128, 4096], P(None, 'gx', 'gy'), may hold values from -500 to 500
- potential: float32 [128, 4096], P('gx', 'gy'), may hold values from -2 to 0
Outputs:
- orbitals: float32 [64, 128, 4096], P(None, 'gx', 'gy')
All inputs are finite; a program needn't handle non-finite values.
Results may differ from a plain program's by a relative error of at most 0.0003.
Values sent between devices are 32-bit elements; how exact they have to be, the bound alone decides.
No kernel may reach another device: no remote copies, remote signals or barrier semaphores. Data moves between devices by JAX's collectives and lax.ppermute only.
A program may use at most 64 MiB of HBM per device.

v0:
```python
import jax
import jax.numpy as jnp
from jax import lax
from jax.sharding import PartitionSpec as P

NZ = 64
COEFS = (-205.0 / 72.0, 8.0 / 5.0, -1.0 / 5.0, 8.0 / 315.0, -1.0 / 560.0)
CENTER = 6.5
HALF_WIDTH = 5.5


def padded(array, sides, width):
    for axis, dim in sides:
        size, length = (lax.axis_size(axis), array.shape[dim])
        up = [(i, (i + 1) % size) for i in range(size)]
        down = [(j, i) for i, j in up]
        last = lax.slice_in_dim(array, length - width, length, axis=dim)
        first = lax.slice_in_dim(array, 0, width, axis=dim)
        before = lax.ppermute(last, axis, up)
        after = lax.ppermute(first, axis, down)
        array = jnp.concatenate([before, array, after], axis=dim)
    return array


def along_third(field, depth_index):
    laplace = 3.0 * COEFS[0] * field
    for distance in range(1, 5):
        forward = jnp.where(
            depth_index < NZ - distance,
            jnp.roll(field, -distance, 2),
            jnp.roll(field, NZ - distance, 2),
        )
        behind = jnp.where(
            depth_index >= distance, jnp.roll(field, distance, 2), jnp.roll(field, distance - NZ, 2)
        )
        laplace = laplace + COEFS[distance] * (forward + behind)
    return laplace


def hamiltonian(field, field_pot, depth_index):
    row_count = field.shape[1]
    lane_count = field.shape[2]
    padded_x = padded(field, (("gx", 1),), 4)
    laplace = along_third(field, depth_index)
    padded_y = padded(field, (("gy", 2),), 4 * NZ)
    for distance in range(1, 5):
        laplace = laplace + COEFS[distance] * (
            padded_x[:, 4 + distance : 4 + distance + row_count]
            + padded_x[:, 4 - distance : 4 - distance + row_count]
        )
        ahead_start = (4 + distance) * NZ
        back_start = (4 - distance) * NZ
        laplace = laplace + COEFS[distance] * (
            padded_y[:, :, ahead_start : ahead_start + lane_count]
            + padded_y[:, :, back_start : back_start + lane_count]
        )
    return -0.5 * laplace + field_pot * field


def orthonormal(matrix, ncount):
    local_gram = jnp.dot(matrix, matrix.T, precision=lax.Precision.HIGHEST) / ncount
    total_gram = lax.psum(local_gram, ("gx", "gy"))
    lower_factor = jnp.linalg.cholesky(total_gram)
    return lax.linalg.triangular_solve(lower_factor, matrix, left_side=True, lower=True)


def on_device(psi, potential):
    orbit_count = psi.shape[0]
    row_count = psi.shape[1]
    lane_count = psi.shape[2]
    field_pot = potential.reshape(1, row_count, lane_count)
    depth_index = lax.broadcasted_iota(jnp.int32, (1, 1, lane_count), 2) % NZ
    level_one = (hamiltonian(psi, field_pot, depth_index) - CENTER * psi) / HALF_WIDTH
    second = (
        2.0 * (hamiltonian(level_one, field_pot, depth_index) - CENTER * level_one) / HALF_WIDTH
        - psi
    )
    filtered = (
        2.0 * (hamiltonian(second, field_pot, depth_index) - CENTER * second) / HALF_WIDTH
        - level_one
    )
    matrix = filtered.reshape(orbit_count, row_count * lane_count)
    ncount = float(row_count * lane_count * lax.axis_size("gx") * lax.axis_size("gy"))
    first_pass = orthonormal(matrix, ncount)
    final_pass = orthonormal(first_pass, ncount)
    return final_pass.reshape(orbit_count, row_count, lane_count)


def solution(mesh):
    in_specs = (P(None, "gx", "gy"), P("gx", "gy"))
    out_specs = P(None, "gx", "gy")
    return jax.shard_map(
        on_device, mesh=mesh, in_specs=in_specs, out_specs=out_specs, check_vma=False
    )
```

profile of v0, /device:TPU:1, one launch (start us, length us, event | category | flops | bytes accessed | tf_op | source)
XLA Modules:
  0.0 262.9 jit_solution(8503108184494606311)
XLA Ops:
  0.0 2.6 collective-permute-start.3
  2.6 0.6 collective-permute-start.2
  3.2 1.3 fusion.198
  4.5 6.0 %collective-permute-start = (f32[64,4,256]{2,1,0:T(4,128)S(1)}, f32[64,4,256]{2,1,0:T(4,128)S(1)}, u32[]{:S(2)}, u32[]{:S(2)}) collective-permute-start(f32[64,4,256]{2,1,0:T(4,128)S(1)} %get-tuple-element.112), channel_id=1, source_target_pairs={{16,0},{32,16},{48,32},{64,48},{80,64},{96,80},{112,96},{128,112},... | collective-permute-start | bytes 786440 | tf_op jit(solution)/shard_map/ppermute | solution.py:20
  14.2 6.1 %collective-permute-done = f32[64,4,256]{2,1,0:T(4,128)S(1)} collective-permute-done((f32[64,4,256]{2,1,0:T(4,128)S(1)}, f32[64,4,256]{2,1,0:T(4,128)S(1)}, u32[]{:S(2)}, u32[]{:S(2)}) %collective-permute-start) | collective-permute-done | bytes 262176 | tf_op jit(solution)/shard_map/ppermute | solution.py:20
  20.4 3.0 %collective-permute-done.1 = f32[64,4,256]{2,1,0:T(4,128)S(1)} collective-permute-done((f32[64,4,256]{2,1,0:T(4,128)S(1)}, f32[64,4,256]{2,1,0:T(4,128)S(1)}, u32[]{:S(2)}, u32[]{:S(2)}) %collective-permute-start.1) | collective-permute-done | bytes 262176 | tf_op jit(solution)/shard_map/ppermute | solution.py:19
  23.4 3.3 %broadcast_multiply_fusion = (f32[64,8,256]{2,1,0:T(8,128)S(1)}, f32[64,8,256]{2,1,0:T(8,128)S(1)}) fusion(f32[64,8,256]{2,1,0:T(8,128)S(1)} %copy-done, f32[8,256]{1,0:T(8,128)S(1)} %copy-done.1, f32[64,8,256]{2,1,0:T(8,128)S(1)} %collective-permute-done.2, f32[64,8,256]{2,1,0:T(8,128)S(1)} %collective-permute-done.3, ...), kind=kLoop, calls=%fused_computation.221 | loop fusion | flops 9306112 | bytes 16525312 | tf_op jit(solution)/shard_map/div | solution.py:73
  29.2 1.5 collective-permute-start.6
  31.0 6.1 %collective-permute-start.4 = (f32[64,4,256]{2,1,0:T(4,128)S(1)}, f32[64,4,256]{2,1,0:T(4,128)S(1)}, u32[]{:S(2)}, u32[]{:S(2)}) collective-permute-start(f32[64,4,256]{2,1,0:T(4,128)S(1)} %get-tuple-element.75), channel_id=1, source_target_pairs={{16,0},{32,16},{48,32},{64,48},{80,64},{96,80},{112,96},{128,112},... | collective-permute-start | bytes 786440 | tf_op jit(solution)/shard_map/ppermute | solution.py:20
  37.5 3.5 %collective-permute-done.4 = f32[64,4,256]{2,1,0:T(4,128)S(1)} collective-permute-done((f32[64,4,256]{2,1,0:T(4,128)S(1)}, f32[64,4,256]{2,1,0:T(4,128)S(1)}, u32[]{:S(2)}, u32[]{:S(2)}) %collective-permute-start.4) | collective-permute-done | bytes 262176 | tf_op jit(solution)/shard_map/ppermute | solution.py:20
  41.0 10.6 %collective-permute-done.5 = f32[64,4,256]{2,1,0:T(4,128)S(1)} collective-permute-done((f32[64,4,256]{2,1,0:T(4,128)S(1)}, f32[64,4,256]{2,1,0:T(4,128)S(1)}, u32[]{:S(2)}, u32[]{:S(2)}) %collective-permute-start.5) | collective-permute-done | bytes 262176 | tf_op jit(solution)/shard_map/ppermute | solution.py:19
  51.6 3.7 %fusion.33 = f32[64,8,256]{2,1,0:T(8,128)S(1)} fusion(f32[64,8,256]{2,1,0:T(8,128)S(1)} %copy-done, f32[64,8,256]{2,1,0:T(8,128)S(1)} %collective-permute-done.7, f32[64,8,256]{2,1,0:T(8,128)S(1)} %get-tuple-element.6, f32[64,8,256]{2,1,0:T(8,128)S(1)} %collective-permute-done.6, f32[64,4,256]{2,1,0:T(4,128)S(1)} %collective-permute-done.5, ...), kind=kLoop, calls=%fused_computation.81 | loop fusion | flops 10747904 | bytes 12068864 | tf_op jit(solution)/shard_map/sub | solution.py:75
  56.6 1.3 collective-permute-start.10
  59.5 4.7 %collective-permute-start.8 = (f32[64,4,256]{2,1,0:T(4,128)S(1)}, f32[64,4,256]{2,1,0:T(4,128)S(1)}, u32[]{:S(2)}, u32[]{:S(2)}) collective-permute-start(f32[64,4,256]{2,1,0:T(4,128)S(1)} %get-tuple-element.41), channel_id=1, source_target_pairs={{16,0},{32,16},{48,32},{64,48},{80,64},{96,80},{112,96},{128,112},... | collective-permute-start | bytes 786440 | tf_op jit(solution)/shard_map/ppermute | solution.py:20
  64.7 3.0 %collective-permute-done.8 = f32[64,4,256]{2,1,0:T(4,128)S(1)} collective-permute-done((f32[64,4,256]{2,1,0:T(4,128)S(1)}, f32[64,4,256]{2,1,0:T(4,128)S(1)}, u32[]{:S(2)}, u32[]{:S(2)}) %collective-permute-start.8) | collective-permute-done | bytes 262176 | tf_op jit(solution)/shard_map/ppermute | solution.py:20
  67.6 12.3 %collective-permute-done.9 = f32[64,4,256]{2,1,0:T(4,128)S(1)} collective-permute-done((f32[64,4,256]{2,1,0:T(4,128)S(1)}, f32[64,4,256]{2,1,0:T(4,128)S(1)}, u32[]{:S(2)}, u32[]{:S(2)}) %collective-permute-start.9) | collective-permute-done | bytes 262176 | tf_op jit(solution)/shard_map/ppermute | solution.py:19
  80.0 3.7 %fusion.13 = f32[64,8,256]{2,1,0:T(8,128)S(1)} fusion(f32[64,8,256]{2,1,0:T(8,128)S(1)} %collective-permute-done.11, f32[64,8,256]{2,1,0:T(8,128)S(1)} %fusion.33, f32[64,8,256]{2,1,0:T(8,128)S(1)} %collective-permute-done.10, f32[64,4,256]{2,1,0:T(4,128)S(1)} %collective-permute-done.9, f32[64,4,256]{2,1,0:T(4,128)S(1)} %collective-permute-done.8, ...), kind=kLoop, calls=%fused_computation.61 | loop fusion | flops 10878976 | bytes 11544576 | tf_op jit(solution)/shard_map/sub | solution.py:79
  83.7 0.7 fusion
  84.4 78.3 %psum.14 = f32[64,64]{0,1:T(8,128)S(1)} all-reduce(f32[64,64]{0,1:T(8,128)S(1)} %fusion), channel_id=1, replica_groups=mesh['gx'=16,'gy'=16] {'gx','gy'}, use_global_device_ids=true, to_apply=%region_0.1 | all-reduce | flops 4096 | bytes 32768 | tf_op jit(solution)/shard_map/psum | solution.py:62
  162.9 5.8 %cholesky.44 = f32[64,64]{1,0:T(8,128)S(1)} custom-call(f32[64,64]{1,0:T(8,128)S(1)} %fusion.144), custom_call_target="Cholesky" | custom-call | tf_op jit(solution)/shard_map/jit(cholesky)/cholesky | solution.py:63
  168.7 0.6 compare_reduce_fusion.1
  169.4 0.7 fusion.137
  170.0 4.9 %custom-call.6 = f32[1,64,64]{1,2,0:T(8,128)S(1)} custom-call(f32[1,64,64]{2,1,0:T(8,128)S(1)} %fusion.137), custom_call_target="InvertDiagBlocksLowerTriangular" | custom-call | tf_op jit(solution)/shard_map/triangular_solve/custom-call.0 | solution.py:64
  175.1 0.6 fusion.142
  175.8 0.6 convolution_multiply_fusion
  176.3 72.7 %psum.15 = f32[64,64]{0,1:T(8,128)S(1)} all-reduce(f32[64,64]{0,1:T(8,128)S(1)} %convolution_multiply_fusion), channel_id=1, replica_groups=mesh['gx'=16,'gy'=16] {'gx','gy'}, use_global_device_ids=true, to_apply=%region_3.6 | all-reduce | flops 4096 | bytes 32768 | tf_op jit(solution)/shard_map/psum | solution.py:62
  249.2 5.8 %cholesky.55 = f32[64,64]{1,0:T(8,128)S(1)} custom-call(f32[64,64]{1,0:T(8,128)S(1)} %fusion.141), custom_call_target="Cholesky" | custom-call | tf_op jit(solution)/shard_map/jit(cholesky)/cholesky | solution.py:63
  255.0 0.6 compare_reduce_fusion
  255.7 0.7 fusion.138
  256.4 4.9 %custom-call.7 = f32[1,64,64]{1,2,0:T(8,128)S(1)} custom-call(f32[1,64,64]{2,1,0:T(8,128)S(1)} %fusion.138), custom_call_target="InvertDiagBlocksLowerTriangular" | custom-call | tf_op jit(solution)/shard_map/triangular_solve/custom-call.0 | solution.py:64
  261.2 0.6 fusion.139
  261.9 1.0 copy.13
  (81 shorter events, 10.4 us)
Async XLA Ops:
  0.0 10.6 %copy-start = (f32[64,8,256]{2,1,0:T(8,128)S(1)}, f32[64,8,256]{2,1,0:T(8,128)}, u32[]{:S(2)}) copy-start(f32[64,8,256]{2,1,0:T(8,128)} %param.5) | copy-start | bytes 1572868
  0.0 13.9 %collective-permute-start.3 = (f32[64,8,256]{2,1,0:T(8,128)}, f32[64,8,256]{2,1,0:T(8,128)S(1)}, u32[]{:S(2)}, u32[]{:S(2)}) collective-permute-start(f32[64,8,256]{2,1,0:T(8,128)} %param.5), channel_id=1, source_target_pairs={{0,1},{1,2},{2,3},{3,4},{4,5},{5,6},{6,7},{7,8},{8,9},{9,10},{10,1... | collective-permute-start | bytes 1572872 | tf_op jit(solution)/shard_map/ppermute | solution.py:19
  2.6 17.7 %collective-permute-start.2 = (f32[64,8,256]{2,1,0:T(8,128)}, f32[64,8,256]{2,1,0:T(8,128)S(1)}, u32[]{:S(2)}, u32[]{:S(2)}) collective-permute-start(f32[64,8,256]{2,1,0:T(8,128)} %param.5), channel_id=1, source_target_pairs={{1,0},{2,1},{3,2},{4,3},{5,4},{6,5},{7,6},{8,7},{9,8},{10,9},{11,1... | collective-permute-start | bytes 1572872 | tf_op jit(solution)/shard_map/ppermute | solution.py:20
  4.5 15.7 %collective-permute-start = (f32[64,4,256]{2,1,0:T(4,128)S(1)}, f32[64,4,256]{2,1,0:T(4,128)S(1)}, u32[]{:S(2)}, u32[]{:S(2)}) collective-permute-start(f32[64,4,256]{2,1,0:T(4,128)S(1)} %get-tuple-element.112), channel_id=1, source_target_pairs={{16,0},{32,16},{48,32},{64,48},{80,64},{96,80},{112,96},{128,112},... | collective-permute-start | bytes 786440 | tf_op jit(solution)/shard_map/ppermute | solution.py:20
  10.6 12.9 %collective-permute-start.1 = (f32[64,4,256]{2,1,0:T(4,128)S(1)}, f32[64,4,256]{2,1,0:T(4,128)S(1)}, u32[]{:S(2)}, u32[]{:S(2)}) collective-permute-start(f32[64,4,256]{2,1,0:T(4,128)S(1)} %get-tuple-element.113), channel_id=1, source_target_pairs={{0,16},{16,32},{32,48},{48,64},{64,80},{80,96},{96,112},{112,128},... | collective-permute-start | bytes 786440 | tf_op jit(solution)/shard_map/ppermute | solution.py:19
  13.0 0.7 copy-start.1
  29.2 22.3 %collective-permute-start.6 = (f32[64,8,256]{2,1,0:T(8,128)S(1)}, f32[64,8,256]{2,1,0:T(8,128)S(1)}, u32[]{:S(2)}, u32[]{:S(2)}) collective-permute-start(f32[64,8,256]{2,1,0:T(8,128)S(1)} %get-tuple-element.6), channel_id=1, source_target_pairs={{1,0},{2,1},{3,2},{4,3},{5,4},{6,5},{7,6},{8,7},{9,8},{10,9},{11,1... | collective-permute-start | bytes 1572872 | tf_op jit(solution)/shard_map/ppermute | solution.py:20
  30.7 20.9 %collective-permute-start.7 = (f32[64,8,256]{2,1,0:T(8,128)S(1)}, f32[64,8,256]{2,1,0:T(8,128)S(1)}, u32[]{:S(2)}, u32[]{:S(2)}) collective-permute-start(f32[64,8,256]{2,1,0:T(8,128)S(1)} %get-tuple-element.6), channel_id=1, source_target_pairs={{0,1},{1,2},{2,3},{3,4},{4,5},{5,6},{6,7},{7,8},{8,9},{9,10},{10,1... | collective-permute-start | bytes 1572872 | tf_op jit(solution)/shard_map/ppermute | solution.py:19
  31.0 10.0 %collective-permute-start.4 = (f32[64,4,256]{2,1,0:T(4,128)S(1)}, f32[64,4,256]{2,1,0:T(4,128)S(1)}, u32[]{:S(2)}, u32[]{:S(2)}) collective-permute-start(f32[64,4,256]{2,1,0:T(4,128)S(1)} %get-tuple-element.75), channel_id=1, source_target_pairs={{16,0},{32,16},{48,32},{64,48},{80,64},{96,80},{112,96},{128,112},... | collective-permute-start | bytes 786440 | tf_op jit(solution)/shard_map/ppermute | solution.py:20
  37.1 14.5 %collective-permute-start.5 = (f32[64,4,256]{2,1,0:T(4,128)S(1)}, f32[64,4,256]{2,1,0:T(4,128)S(1)}, u32[]{:S(2)}, u32[]{:S(2)}) collective-permute-start(f32[64,4,256]{2,1,0:T(4,128)S(1)} %get-tuple-element.76), channel_id=1, source_target_pairs={{0,16},{16,32},{32,48},{48,64},{64,80},{80,96},{96,112},{112,128},... | collective-permute-start | bytes 786440 | tf_op jit(solution)/shard_map/ppermute | solution.py:19
  56.6 23.4 %collective-permute-start.10 = (f32[64,8,256]{2,1,0:T(8,128)S(1)}, f32[64,8,256]{2,1,0:T(8,128)S(1)}, u32[]{:S(2)}, u32[]{:S(2)}) collective-permute-start(f32[64,8,256]{2,1,0:T(8,128)S(1)} %fusion.33), channel_id=1, source_target_pairs={{1,0},{2,1},{3,2},{4,3},{5,4},{6,5},{7,6},{8,7},{9,8},{10,9},{11,1... | collective-permute-start | bytes 1572872 | tf_op jit(solution)/shard_map/ppermute | solution.py:20
  57.9 22.1 %collective-permute-start.11 = (f32[64,8,256]{2,1,0:T(8,128)S(1)}, f32[64,8,256]{2,1,0:T(8,128)S(1)}, u32[]{:S(2)}, u32[]{:S(2)}) collective-permute-start(f32[64,8,256]{2,1,0:T(8,128)S(1)} %fusion.33), channel_id=1, source_target_pairs={{0,1},{1,2},{2,3},{3,4},{4,5},{5,6},{6,7},{7,8},{8,9},{9,10},{10,1... | collective-permute-start | bytes 1572872 | tf_op jit(solution)/shard_map/ppermute | solution.py:19
  59.5 8.1 %collective-permute-start.8 = (f32[64,4,256]{2,1,0:T(4,128)S(1)}, f32[64,4,256]{2,1,0:T(4,128)S(1)}, u32[]{:S(2)}, u32[]{:S(2)}) collective-permute-start(f32[64,4,256]{2,1,0:T(4,128)S(1)} %get-tuple-element.41), channel_id=1, source_target_pairs={{16,0},{32,16},{48,32},{64,48},{80,64},{96,80},{112,96},{128,112},... | collective-permute-start | bytes 786440 | tf_op jit(solution)/shard_map/ppermute | solution.py:20
  64.2 15.7 %collective-permute-start.9 = (f32[64,4,256]{2,1,0:T(4,128)S(1)}, f32[64,4,256]{2,1,0:T(4,128)S(1)}, u32[]{:S(2)}, u32[]{:S(2)}) collective-permute-start(f32[64,4,256]{2,1,0:T(4,128)S(1)} %get-tuple-element.42), channel_id=1, source_target_pairs={{0,16},{16,32},{32,48},{48,64},{64,80},{80,96},{96,112},{112,128},... | collective-permute-start | bytes 786440 | tf_op jit(solution)/shard_map/ppermute | solution.py:19
where the time goes:
time: 263 us
  blocking collectives  151 us (57%)
  waiting for transfers between devices  38.5 us (15%)
  other arithmetic  35 us (13%)
  starting transfers between devices  23.7 us (9%)
  local copies, waits for them, and re-layouts  11.6 us (4%)
    psum x2, blocking collectives, orthonormal(): total_gram = lax.psum(local_gram, ('gx', 'gy'))  151 us
    ppermute x6, waiting for transfers between devices, padded(): before = lax.ppermute(last, axis, up)  25.9 us
    ppermute x6, starting transfers between devices, padded(): after = lax.ppermute(first, axis, down)  20.2 us
    another operation x6, other arithmetic, orthonormal(): lower_factor = jnp.linalg.cholesky(total_gram)  13 us
    ppermute x6, waiting for transfers between devices, padded(): after = lax.ppermute(first, axis, down)  12.5 us
    another operation x4, other arithmetic, orthonormal(): lax.linalg.triangular_solve(lower_factor, matrix, left_side=True, lower=T...  11.1 us
  transfers between devices with their start and end apart: 12, of which 6 were waited for; matrix products, arithmetic and copies ran while one was open for 2% of the time, Pallas kernels for 0%

commit v1 on v0

--- a/solution.py
+++ b/solution.py
@@ -59,7 +59,7 @@
 
 def orthonormal(matrix, ncount):
     local_gram = jnp.dot(matrix, matrix.T, precision=lax.Precision.HIGHEST) / ncount
-    total_gram = lax.psum(local_gram, ("gx", "gy"))
+    total_gram = jnp.sum(lax.all_gather(local_gram, ("gx", "gy")), axis=0)
     lower_factor = jnp.linalg.cholesky(total_gram)
     return lax.linalg.triangular_solve(lower_factor, matrix, left_side=True, lower=True)
 

time: 263 us -> 970 us (3.69)
  waiting for transfers between devices: 38.5 us -> 869 us
  blocking collectives: 151 us -> 0 us
  between operations: 0.39 us -> 13.8 us
    all_gather x0 -> x2, waiting for transfers between devices: none -> 835 us  [orthonormal(): total_gram = jnp.sum(lax.all_gather(local_gram, ('gx', 'gy')), axis=0)]
    psum x2 -> x0, blocking collectives: 151 us -> none  [orthonormal(): total_gram = lax.psum(local_gram, ('gx', 'gy'))]
  transfers between devices with their start and end apart: 12 -> 14, of which waited for: 6 -> 8; matrix products, arithmetic and copies ran while one was open for 2% -> 1% of each run, Pallas kernels for 0% -> 0%
where the time goes in v1:
time: 970 us; the launch traced here: 969 us
  waiting for transfers between devices  869 us (90%)
  other arithmetic  43 us (4%)
  starting transfers between devices  24 us (2%)
  local copies, waits for them, and re-layouts  15.9 us (2%)
  between operations  13.8 us (1%)
    all_gather x2, waiting for transfers between devices, orthonormal(): total_gram = jnp.sum(lax.all_gather(local_gram, ('gx', 'gy')), axis=0)  835 us
    ppermute x6, waiting for transfers between devices, padded(): before = lax.ppermute(last, axis, up)  25.9 us
    ppermute x6, starting transfers between devices, padded(): after = lax.ppermute(first, axis, down)  20.2 us
  transfers between devices with their start and end apart: 14, of which 8 were waited for; matrix products, arithmetic and copies ran while one was open for 1% of the time, Pallas kernels for 0%

profile of v1, /device:TPU:1, one launch (start us, length us, event | category | flops | bytes accessed | tf_op | source)
XLA Modules:
  0.0 969.5 jit_solution(15425333245427688819)
XLA Ops:
  6.5 2.6 collective-permute-start.3
  9.8 1.3 fusion.198
  11.1 6.0 collective-permute-start
  17.1 1.4 fusion.193
  18.5 1.4 fusion.194
  20.0 1.4 fusion.197
  21.4 1.4 fusion.182
  25.0 1.8 collective-permute-done
  27.0 3.0 collective-permute-done.1
  30.0 3.3 broadcast_multiply_fusion
  35.7 1.5 collective-permute-start.6
  37.6 6.1 collective-permute-start.4
  44.1 3.5 collective-permute-done.4
  47.6 10.5 %collective-permute-done.5 = f32[64,4,256]{2,1,0:T(4,128)S(1)} collective-permute-done((f32[64,4,256]{2,1,0:T(4,128)S(1)}, f32[64,4,256]{2,1,0:T(4,128)S(1)}, u32[]{:S(2)}, u32[]{:S(2)}) %collective-permute-start.5) | collective-permute-done | bytes 262176 | tf_op jit(solution)/shard_map/ppermute | solution.py:19
  58.1 3.7 fusion.33
  63.2 1.3 collective-permute-start.10
  66.1 4.7 collective-permute-start.8
  71.2 3.0 collective-permute-done.8
  74.2 12.4 %collective-permute-done.9 = f32[64,4,256]{2,1,0:T(4,128)S(1)} collective-permute-done((f32[64,4,256]{2,1,0:T(4,128)S(1)}, f32[64,4,256]{2,1,0:T(4,128)S(1)}, u32[]{:S(2)}, u32[]{:S(2)}) %collective-permute-start.9) | collective-permute-done | bytes 262176 | tf_op jit(solution)/shard_map/ppermute | solution.py:19
  86.5 3.7 fusion.13
  90.3 1.3 fusion
  92.0 417.7 %all-gather.5.cloned.1.call-done = f32[16384,64]{1,0:T(8,128)} async-done(((f32[64,64]{1,0:T(8,128)}), f32[16384,64]{1,0:T(8,128)}) %all-gather.5.cloned.1.call-update) | async-done | bytes 4194320 | tf_op jit(solution)/shard_map/all_gather | solution.py:62
  509.8 4.0 reduce_sum.18
  513.9 5.8 cholesky.44
  520.4 0.7 fusion.137
  521.0 4.9 custom-call.6
  526.6 1.2 convolution_multiply_fusion
  527.8 417.0 %all-gather.7.cloned.1.call-done = f32[16384,64]{1,0:T(8,128)} async-done(((f32[64,64]{1,0:T(8,128)}), f32[16384,64]{1,0:T(8,128)}) %all-gather.7.cloned.1.call-update) | async-done | bytes 4194320 | tf_op jit(solution)/shard_map/all_gather | solution.py:62
  944.8 4.0 reduce_sum.19
  948.9 5.8 cholesky.55
  956.1 4.9 custom-call.7
  961.7 1.0 copy.12
  (87 shorter events, 13.2 us)
Async XLA Ops:
  6.5 16.3 %copy-start = (f32[64,8,256]{2,1,0:T(8,128)S(1)}, f32[64,8,256]{2,1,0:T(8,128)}, u32[]{:S(2)}) copy-start(f32[64,8,256]{2,1,0:T(8,128)} %param.5) | copy-start | bytes 1572868
  6.5 503.2 %all-gather.5.cloned.1.call-start = ((), (), s32[]{:S(2)}) async-start(), calls=%async_computation | async-start | bytes 8421376 | tf_op jit(solution)/shard_map/all_gather | solution.py:62
  6.5 18.2 %collective-permute-start.3 = (f32[64,8,256]{2,1,0:T(8,128)}, f32[64,8,256]{2,1,0:T(8,128)S(1)}, u32[]{:S(2)}, u32[]{:S(2)}) collective-permute-start(f32[64,8,256]{2,1,0:T(8,128)} %param.5), channel_id=1, source_target_pairs={{0,1},{1,2},{2,3},{3,4},{4,5},{5,6},{6,7},{7,8},{8,9},{9,10},{10,1... | collective-permute-start | bytes 1572872 | tf_op jit(solution)/shard_map/ppermute | solution.py:19
  9.1 17.8 %collective-permute-start.2 = (f32[64,8,256]{2,1,0:T(8,128)}, f32[64,8,256]{2,1,0:T(8,128)S(1)}, u32[]{:S(2)}, u32[]{:S(2)}) collective-permute-start(f32[64,8,256]{2,1,0:T(8,128)} %param.5), channel_id=1, source_target_pairs={{1,0},{2,1},{3,2},{4,3},{5,4},{6,5},{7,6},{8,7},{9,8},{10,9},{11,1... | collective-permute-start | bytes 1572872 | tf_op jit(solution)/shard_map/ppermute | solution.py:20
  11.1 15.7 %collective-permute-start = (f32[64,4,256]{2,1,0:T(4,128)S(1)}, f32[64,4,256]{2,1,0:T(4,128)S(1)}, u32[]{:S(2)}, u32[]{:S(2)}) collective-permute-start(f32[64,4,256]{2,1,0:T(4,128)S(1)} %get-tuple-element.112), channel_id=1, source_target_pairs={{16,0},{32,16},{48,32},{64,48},{80,64},{96,80},{112,96},{128,112},... | collective-permute-start | bytes 786440 | tf_op jit(solution)/shard_map/ppermute | solution.py:20
  17.1 12.9 %collective-permute-start.1 = (f32[64,4,256]{2,1,0:T(4,128)S(1)}, f32[64,4,256]{2,1,0:T(4,128)S(1)}, u32[]{:S(2)}, u32[]{:S(2)}) collective-permute-start(f32[64,4,256]{2,1,0:T(4,128)S(1)} %get-tuple-element.113), channel_id=1, source_target_pairs={{0,16},{16,32},{32,48},{48,64},{64,80},{80,96},{96,112},{112,128},... | collective-permute-start | bytes 786440 | tf_op jit(solution)/shard_map/ppermute | solution.py:19
  21.4 3.1 copy-start.1
  35.7 22.4 %collective-permute-start.6 = (f32[64,8,256]{2,1,0:T(8,128)S(1)}, f32[64,8,256]{2,1,0:T(8,128)S(1)}, u32[]{:S(2)}, u32[]{:S(2)}) collective-permute-start(f32[64,8,256]{2,1,0:T(8,128)S(1)} %get-tuple-element.6), channel_id=1, source_target_pairs={{1,0},{2,1},{3,2},{4,3},{5,4},{6,5},{7,6},{8,7},{9,8},{10,9},{11,1... | collective-permute-start | bytes 1572872 | tf_op jit(solution)/shard_map/ppermute | solution.py:20
  37.2 20.9 %collective-permute-start.7 = (f32[64,8,256]{2,1,0:T(8,128)S(1)}, f32[64,8,256]{2,1,0:T(8,128)S(1)}, u32[]{:S(2)}, u32[]{:S(2)}) collective-permute-start(f32[64,8,256]{2,1,0:T(8,128)S(1)} %get-tuple-element.6), channel_id=1, source_target_pairs={{0,1},{1,2},{2,3},{3,4},{4,5},{5,6},{6,7},{7,8},{8,9},{9,10},{10,1... | collective-permute-start | bytes 1572872 | tf_op jit(solution)/shard_map/ppermute | solution.py:19
  37.6 10.0 %collective-permute-start.4 = (f32[64,4,256]{2,1,0:T(4,128)S(1)}, f32[64,4,256]{2,1,0:T(4,128)S(1)}, u32[]{:S(2)}, u32[]{:S(2)}) collective-permute-start(f32[64,4,256]{2,1,0:T(4,128)S(1)} %get-tuple-element.75), channel_id=1, source_target_pairs={{16,0},{32,16},{48,32},{64,48},{80,64},{96,80},{112,96},{128,112},... | collective-permute-start | bytes 786440 | tf_op jit(solution)/shard_map/ppermute | solution.py:20
  43.7 14.5 %collective-permute-start.5 = (f32[64,4,256]{2,1,0:T(4,128)S(1)}, f32[64,4,256]{2,1,0:T(4,128)S(1)}, u32[]{:S(2)}, u32[]{:S(2)}) collective-permute-start(f32[64,4,256]{2,1,0:T(4,128)S(1)} %get-tuple-element.76), channel_id=1, source_target_pairs={{0,16},{16,32},{32,48},{48,64},{64,80},{80,96},{96,112},{112,128},... | collective-permute-start | bytes 786440 | tf_op jit(solution)/shard_map/ppermute | solution.py:19
  63.2 23.4 %collective-permute-start.10 = (f32[64,8,256]{2,1,0:T(8,128)S(1)}, f32[64,8,256]{2,1,0:T(8,128)S(1)}, u32[]{:S(2)}, u32[]{:S(2)}) collective-permute-start(f32[64,8,256]{2,1,0:T(8,128)S(1)} %fusion.33), channel_id=1, source_target_pairs={{1,0},{2,1},{3,2},{4,3},{5,4},{6,5},{7,6},{8,7},{9,8},{10,9},{11,1... | collective-permute-start | bytes 1572872 | tf_op jit(solution)/shard_map/ppermute | solution.py:20
  64.4 22.1 %collective-permute-start.11 = (f32[64,8,256]{2,1,0:T(8,128)S(1)}, f32[64,8,256]{2,1,0:T(8,128)S(1)}, u32[]{:S(2)}, u32[]{:S(2)}) collective-permute-start(f32[64,8,256]{2,1,0:T(8,128)S(1)} %fusion.33), channel_id=1, source_target_pairs={{0,1},{1,2},{2,3},{3,4},{4,5},{5,6},{6,7},{7,8},{8,9},{9,10},{10,1... | collective-permute-start | bytes 1572872 | tf_op jit(solution)/shard_map/ppermute | solution.py:19
  66.1 8.1 collective-permute-start.8
  70.8 15.7 %collective-permute-start.9 = (f32[64,4,256]{2,1,0:T(4,128)S(1)}, f32[64,4,256]{2,1,0:T(4,128)S(1)}, u32[]{:S(2)}, u32[]{:S(2)}) collective-permute-start(f32[64,4,256]{2,1,0:T(4,128)S(1)} %get-tuple-element.42), channel_id=1, source_target_pairs={{0,16},{16,32},{32,48},{48,64},{64,80},{80,96},{96,112},{112,128},... | collective-permute-start | bytes 786440 | tf_op jit(solution)/shard_map/ppermute | solution.py:19
  91.6 853.2 %all-gather.7.cloned.1.call-start = ((), (), s32[]{:S(2)}) async-start(), calls=%async_computation.1 | async-start | bytes 8421376 | tf_op jit(solution)/shard_map/all_gather | solution.py:62
Sparse Core Ops, SparseCore 0:
  91.7 417.9 all-gather.4
  527.9 416.8 all-gather.6
